TPU v7x, 32 devices: a whole 2x2x4 slice. The times are simulated.
32 devices in a mesh: groups: 2 (over y), ep: 8 (over z, x), tp: 2 (over core).
Axes of the slice: x: 2, y: 2, z: 4, core: 2. Of those that a mesh axis runs over, the one named last changes fastest.
Arguments:
- hidden: bfloat16 [128, 4096], P(('groups', 'ep', 'tp')), parts along dimension 0, may hold values from -6 to 6
- norm_gain: float32 [4096], replicated, may hold values from 0.5 to 1.5
- rot_left: float32 [64, 64], replicated, may hold values from -0.75 to 0.75
- rot_right: float32 [64, 64], replicated, may hold values from -0.75 to 0.75
- expert_ids: int32 [128, 8], P(('groups', 'ep')), parts along dimension 0, may hold values from 0 to 63, as said below
- gate_weights: float32 [128, 8], P(('groups', 'ep')), parts along dimension 0, may hold values from 0.05 to 1
- w_gate: bfloat16 [128, 4096, 384], P('ep', 'tp'), may hold values from -0.09375 to 0.09375
- w_up: bfloat16 [128, 4096, 384], P('ep', 'tp'), may hold values from -0.09375 to 0.09375
- w_down: bfloat16 [128, 384, 4096], P('ep', None, 'tp'), may hold values from -0.21875 to 0.21875
- unit_scales: float32 [128, 2, 384], P('ep'), may hold values from 0.25 to 1.75
Outputs:
- moe_out: bfloat16 [128, 4096], P(('groups', 'ep', 'tp')), parts along dimension 0
There are 2 independent parts, one for each index of `groups`. A program takes and returns all parts, laid end to end along the dimension named above; an argument that names none is the same for every part. Nothing has to cross between parts.
Inputs may be any that keep to these rules, and one draw needn't show every extreme that they name: `expert_ids`: each row names 8 different experts. In each aligned block of 8 rows (the rows of one index of ep) no expert is named by more than 2 rows, and in every block some experts are named by exactly 2 rows; every expert is named by exactly 2 rows in some block.
All inputs are finite; a program needn't handle non-finite values.
Results may differ from a plain program's by a relative error of at most 0.0082.
Values may be sent and summed in bfloat16 or wider, within the bound.
A program may use at most 128 MiB of HBM per device.

v0:
```python
import jax
import jax.numpy as jnp
from jax import lax
from jax.sharding import PartitionSpec as P

EXPERTS = 64


def rotate(hidden, norm_gain, rot_left, rot_right):
    values = hidden.astype(jnp.float32)
    mean_square = jnp.mean(values * values, axis=1, keepdims=True)
    normed = values * lax.rsqrt(mean_square + 1e-06) * norm_gain[None, :]
    factor = rot_left.shape[0]
    square = normed.reshape(-1, factor, factor)
    turned = jnp.einsum("ij,rjk->rik", rot_left, square, precision=lax.Precision.HIGHEST)
    turned = jnp.einsum("rik,lk->ril", turned, rot_right, precision=lax.Precision.HIGHEST)
    return turned.reshape(normed.shape).astype(jnp.bfloat16)


def activate(gate_sum, up_sum, unit_scales):
    gate_scale = unit_scales[None, :, 0, None, :]
    up_scale = unit_scales[None, :, 1, None, :]
    return (jax.nn.silu(gate_sum * gate_scale) * (up_sum * up_scale)).astype(jnp.bfloat16)


def body(
    hidden,
    norm_gain,
    rot_left,
    rot_right,
    expert_ids,
    gate_weights,
    w_gate,
    w_up,
    w_down,
    unit_scales,
):
    ep_count = lax.axis_size("ep")
    group_rows = expert_ids.shape[0]
    top_count = expert_ids.shape[1]
    held_halves = w_gate.shape[0]
    capacity = 5 * group_rows * top_count // (2 * EXPERTS)
    rotated = rotate(hidden, norm_gain, rot_left, rot_right)
    pair_rows = lax.all_to_all(rotated, "tp", split_axis=1, concat_axis=0, tiled=True)
    weight_norm = (gate_weights / jnp.sum(gate_weights, axis=1, keepdims=True)).astype(jnp.bfloat16)
    onehot = (
        expert_ids.reshape(-1)[:, None] == jnp.arange(EXPERTS, dtype=jnp.int32)[None, :]
    ).astype(jnp.int32)
    slot_rank = jnp.sum((jnp.cumsum(onehot, axis=0) - onehot) * onehot, axis=1).reshape(
        group_rows, top_count
    )
    low_target = expert_ids * capacity + slot_rank
    targets = (low_target, low_target + EXPERTS * capacity)
    line_count = 2 * EXPERTS * capacity
    line_index = jnp.arange(line_count, dtype=jnp.int32)[:, None, None]
    matches = jnp.zeros((line_count, group_rows, top_count), jnp.float32)
    for target in targets:
        matches = matches + (line_index == target[None, :, :]).astype(jnp.float32)
    dispatch = jnp.sum(matches, axis=2).astype(jnp.bfloat16)
    outgoing = jnp.dot(dispatch, pair_rows, preferred_element_type=jnp.float32).astype(jnp.bfloat16)
    outgoing = outgoing.reshape(ep_count, held_halves * capacity, -1)
    received = lax.all_to_all(outgoing, "ep", split_axis=0, concat_axis=0, tiled=True)
    received = received.reshape(ep_count, held_halves, capacity, -1)
    gate_sum = jnp.einsum("shcd,hdf->shcf", received, w_gate, preferred_element_type=jnp.float32)
    up_sum = jnp.einsum("shcd,hdf->shcf", received, w_up, preferred_element_type=jnp.float32)
    gate_sum, up_sum = (
        lax.psum_scatter(gate_sum, "tp", scatter_dimension=0, tiled=True),
        lax.psum_scatter(up_sum, "tp", scatter_dimension=0, tiled=True),
    )
    half_hidden = activate(gate_sum, up_sum, unit_scales)
    hidden_units = lax.all_gather(half_hidden, "tp", axis=0, tiled=True)
    partial_value = jnp.einsum(
        "shcf,hfd->shcd", hidden_units, w_down, preferred_element_type=jnp.float32
    ).astype(jnp.bfloat16)
    flat_partial = partial_value.reshape(ep_count, held_halves * capacity, -1)
    returned = lax.all_to_all(flat_partial, "ep", split_axis=0, concat_axis=0, tiled=True)
    returned = returned.reshape(2 * EXPERTS * capacity, -1)
    expert_out = (
        returned[: EXPERTS * capacity].astype(jnp.float32)
        + returned[EXPERTS * capacity :].astype(jnp.float32)
    ).astype(jnp.bfloat16)
    line_spot = (expert_ids * capacity + slot_rank)[:, :, None]
    out_lines = EXPERTS * capacity
    columns = jnp.arange(out_lines, dtype=jnp.int32)[None, None, :]
    hits = (columns == line_spot).astype(jnp.float32)
    mixing = jnp.sum(weight_norm.astype(jnp.float32)[:, :, None] * hits, axis=1).astype(
        jnp.bfloat16
    )
    combined = jnp.dot(mixing, expert_out, preferred_element_type=jnp.float32).astype(jnp.bfloat16)
    return lax.all_to_all(combined, "tp", split_axis=0, concat_axis=1, tiled=True)


def solution(mesh):
    placed = (
        P(("groups", "ep", "tp"), None),
        P(),
        P(),
        P(),
        P(("groups", "ep"), None),
        P(("groups", "ep"), None),
        P("ep", "tp", None),
        P("ep", "tp", None),
        P("ep", None, "tp"),
        P("ep", None, None),
    )
    return jax.shard_map(
        body, mesh=mesh, in_specs=placed, out_specs=P(("groups", "ep", "tp"), None), check_vma=False
    )
```

profile of v0, /device:TPU:0, one launch (start us, length us, event | category | flops | bytes accessed | tf_op | source)
XLA Modules:
  0.0 139.3 jit_solution(9439551862724553802)
XLA Ops:
  6.5 0.0 copy-start
  6.5 0.9 fusion.16
  7.5 0.8 fusion.17
  8.3 0.1 reshape.49
  8.4 0.0 copy-done
  8.4 0.4 convolution_bitcast_fusion
  8.8 1.1 convolution_convert_fusion.2
  10.0 0.1 convert_element_type.70
  10.1 0.6 copy.32
  10.7 3.3 %all-to-all-start = ((bf16[4,2,2048]{2,0,1:T(4,128)(2,1)}), bf16[4,2,2048]{2,0,1:T(4,128)(2,1)S(1)}, u32[]{:S(2)}, u32[]{:S(2)}) async-start(bf16[4,2,2048]{2,0,1:T(4,128)(2,1)} %copy.32), calls=%async_computation | async-start | bytes 65536 | tf_op jit(solution)/shard_map/all_to_all | solution.py:44
  14.0 0.0 reduce-scatter.3.cloned.1.call-start
  14.1 0.8 eq.27
  14.8 0.1 fusion.20
  14.9 0.1 reduce_window_sum.11
  15.0 0.2 select_reduce_fusion.1
  15.2 0.1 reshape.48
  15.3 0.7 broadcast_add_fusion
  16.0 0.0 all-to-all-done
  16.0 0.1 add_reduce_fusion
  16.1 0.5 convolution_convert_fusion
  16.6 33.4 %all_to_all.45 = bf16[8,32,2048]{2,1,0:T(8,128)(2,1)S(1)} all-to-all(bf16[8,32,2048]{2,1,0:T(8,128)(2,1)S(1)} %bitcast.58), channel_id=1, replica_groups=mesh['groups'=2,'ep'=8,'tp'=2] {'ep'}, dimensions={0} | all-to-all | bytes 2097152 | tf_op jit(solution)/shard_map/all_to_all | solution.py:62
  50.0 0.6 copy.33
  50.6 0.0 copy-start.2
  50.6 9.9 %fusion.9 = f32[8,16,2,384]{3,0,2,1:T(8,128)S(1)} fusion(bf16[8,16,2,2048]{3,0,2,1:T(8,128)(2,1)S(1)} %bitcast.55, bf16[16,2048,384]{2,1,0:T(8,128)(2,1)} %param.16), kind=kOutput, calls=%fused_computation.9 | convolution fusion | flops 402653184 | bytes 26607616 | tf_op jit(solution)/shard_map/shcd,hdf->shcf/dot_general | solution.py:64
  60.5 0.9 copy.34
  61.3 0.0 reduce-scatter.3.cloned.1.call-update
  61.4 0.0 reduce-scatter.5.cloned.1.call-start
  61.4 0.0 copy-start.1
  61.4 10.1 %fusion.12 = f32[8,16,2,384]{3,0,2,1:T(8,128)S(1)} fusion(bf16[8,16,2,2048]{3,0,2,1:T(8,128)(2,1)S(1)} %bitcast.56, bf16[16,2048,384]{2,1,0:T(8,128)(2,1)} %param.17), kind=kOutput, calls=%fused_computation.10 | convolution fusion | flops 402653184 | bytes 26607616 | tf_op jit(solution)/shard_map/shcd,hdf->shcf/dot_general | solution.py:65
  71.6 0.0 copy-start.3
  71.6 0.9 copy.36
  72.4 0.0 reduce-scatter.5.cloned.1.call-update
  72.5 0.0 copy-done.2
  72.5 0.0 reduce-scatter.3.cloned.1.call-done
  72.6 7.1 %reduce-scatter.5.cloned.1.call-done = f32[4,16,2,384]{3,1,2,0:T(8,128)} async-done(((f32[8,16,2,384]{3,1,2,0:T(8,128)}), f32[4,16,2,384]{3,1,2,0:T(8,128)}) %reduce-scatter.5.cloned.1.call-update) | async-done | bytes 196624 | tf_op jit(solution)/shard_map/reduce_scatter | solution.py:68
  79.6 1.1 multiply_convert_fusion
  80.7 1.9 %all_gather.3 = bf16[8,16,2,384]{3,1,2,0:T(8,128)(2,1)S(1)} all-gather(bf16[4,16,2,384]{3,1,2,0:T(8,128)(2,1)S(1)} %multiply_convert_fusion), channel_id=1, replica_groups=mesh['groups'=2,'ep'=8,'tp'=2] {'tp'}, dimensions={0}, use_global_device_ids=true | all-gather | bytes 294912 | tf_op jit(solution)/shard_map/all_gather | solution.py:71
  82.7 11.5 %fusion.6 = bf16[16,8,2,2048]{3,1,2,0:T(8,128)(2,1)S(1)} fusion(bf16[16,384,2048]{2,1,0:T(8,128)(2,1)} %param.18, bf16[8,16,2,384]{3,1,2,0:T(8,128)(2,1)S(1)} %all_gather.3), kind=kOutput, calls=%fused_computation.6 | convolution fusion | flops 403177472 | bytes 26411008 | tf_op jit(solution)/shard_map/shcf,hfd->shcd/dot_general | solution.py:72
  94.2 1.6 %copy.39 = bf16[8,32,2048]{2,1,0:T(8,128)(2,1)} copy(bf16[8,32,2048]{2,0,1:T(8,128)(2,1)S(1)} %bitcast.57) | data formatting | bytes 2097152 | tf_op jit(solution)/shard_map/reshape | solution.py:75
  95.8 5.7 %all-to-all-start.2 = ((bf16[8,32,2048]{2,1,0:T(8,128)(2,1)}), bf16[8,32,2048]{2,1,0:T(8,128)(2,1)S(1)}, u32[]{:S(2)}, u32[]{:S(2)}) async-start(bf16[8,32,2048]{2,1,0:T(8,128)(2,1)} %copy.39), calls=%async_computation.4 | async-start | bytes 2097152 | tf_op jit(solution)/shard_map/all_to_all | solution.py:76
  101.5 0.1 reduce_sum.46
  101.6 0.1 fusion.22
  101.7 0.1 select_reduce_fusion
  101.8 26.0 %all-to-all-done.2 = bf16[8,32,2048]{2,1,0:T(8,128)(2,1)S(1)} async-done(((bf16[8,32,2048]{2,1,0:T(8,128)(2,1)}), bf16[8,32,2048]{2,1,0:T(8,128)(2,1)S(1)}, u32[]{:S(2)}, u32[]{:S(2)}) %all-to-all-start.2) | async-done | bytes 1048608 | tf_op jit(solution)/shard_map/all_to_all | solution.py:76
  127.8 0.1 add_convert_fusion
  127.9 0.2 convolution_convert_fusion.1
  128.1 3.7 %all_to_all.46 = bf16[2,4,2048]{2,1,0:T(4,128)(2,1)S(1)} all-to-all(bf16[2,4,2048]{2,1,0:T(4,128)(2,1)S(1)} %all_to_all.37), channel_id=1, replica_groups=mesh['groups'=2,'ep'=8,'tp'=2] {'tp'}, dimensions={0} | all-to-all | bytes 65536 | tf_op jit(solution)/shard_map/all_to_all | solution.py:90
  131.9 0.6 copy.53
  (7 shorter events, 0.1 us)
Async XLA Ops:
  6.5 1.9 %copy-start = (f32[64,64]{1,0:T(8,128)S(1)}, f32[64,64]{1,0:T(8,128)}, u32[]{:S(2)}) copy-start(f32[64,64]{1,0:T(8,128)} %param.12) | copy-start | bytes 49156
  10.7 5.2 %all-to-all-start = ((bf16[4,2,2048]{2,0,1:T(4,128)(2,1)}), bf16[4,2,2048]{2,0,1:T(4,128)(2,1)S(1)}, u32[]{:S(2)}, u32[]{:S(2)}) async-start(bf16[4,2,2048]{2,0,1:T(4,128)(2,1)} %copy.32), calls=%async_computation | async-start | bytes 65536 | tf_op jit(solution)/shard_map/all_to_all | solution.py:44
  14.0 58.5 %reduce-scatter.3.cloned.1.call-start = ((), (), s32[]{:S(2)}) async-start(), calls=%async_computation.6 | async-start | bytes 589824 | tf_op jit(solution)/shard_map/reduce_scatter | solution.py:67
  50.6 21.9 %copy-start.2 = (f32[16,2,384]{2,1,0:T(2,128)S(1)}, f32[16,2,384]{2,1,0:T(2,128)}, u32[]{:S(2)}) copy-start(f32[16,2,384]{2,1,0:T(2,128)} %param.19) | copy-start | bytes 147460
  61.4 18.3 %reduce-scatter.5.cloned.1.call-start = ((), (), s32[]{:S(2)}) async-start(), calls=%async_computation.7 | async-start | bytes 589824 | tf_op jit(solution)/shard_map/reduce_scatter | solution.py:68
  61.4 71.1 %copy-start.1 = (f32[64,64]{1,0:T(8,128)S(1)}, f32[64,64]{1,0:T(8,128)}, u32[]{:S(2)}) copy-start(f32[64,64]{1,0:T(8,128)} %param.12) | copy-start | bytes 49156
  71.6 30.0 %copy-start.3 = (f32[8,8]{1,0:T(8,128)S(1)}, f32[8,8]{1,0:T(8,128)}, u32[]{:S(2)}) copy-start(f32[8,8]{1,0:T(8,128)} %param.15) | copy-start | bytes 772
  95.8 32.0 %all-to-all-start.2 = ((bf16[8,32,2048]{2,1,0:T(8,128)(2,1)}), bf16[8,32,2048]{2,1,0:T(8,128)(2,1)S(1)}, u32[]{:S(2)}, u32[]{:S(2)}) async-start(bf16[8,32,2048]{2,1,0:T(8,128)(2,1)} %copy.39), calls=%async_computation.4 | async-start | bytes 2097152 | tf_op jit(solution)/shard_map/all_to_all | solution.py:76
Sparse Core Ops, SparseCore 0:
  61.5 6.8 reduce-scatter.2
  72.6 7.0 reduce-scatter.4
where the time goes:
time: 140 us; the launch traced here: 139 us
  blocking collectives  39.1 us (28%)
  matrix products  33.7 us (24%)
  waiting for transfers between devices  33.1 us (24%)
  between operations  13.6 us (10%)
  starting transfers between devices  9.08 us (6%)
  local copies, waits for them, and re-layouts  6.33 us (5%)
  other arithmetic  4.44 us (3%)
    all_to_all x1, blocking collectives, body(): lax.all_to_all(outgoing, 'ep', split_axis=0, concat_axis=0, tiled=True)  33.4 us
    all_to_all x1, waiting for transfers between devices, body(): lax.all_to_all(flat_partial, 'ep', split_axis=0, concat_axis=0, tiled=True)  26 us
    dot_general x1, matrix products, body(): jnp.einsum('shcf,hfd->shcd', hidden_units, w_down, preferred_element_type...  11.5 us
    dot_general x1, matrix products, body(): jnp.einsum('shcd,hdf->shcf', received, w_up, preferred_element_type=jnp.f...  10.1 us
    dot_general x1, matrix products, body(): jnp.einsum('shcd,hdf->shcf', received, w_gate, preferred_element_type=jnp...  9.91 us
    reduce_scatter x1, waiting for transfers between devices, body(): lax.psum_scatter(up_sum, 'tp', scatter_dimension=0, tiled=True)  7.08 us
    all_to_all x1, starting transfers between devices, body(): lax.all_to_all(flat_partial, 'ep', split_axis=0, concat_axis=0, tiled=True)  5.74 us
    all_to_all x1, blocking collectives, body(): lax.all_to_all(combined, 'tp', split_axis=0, concat_axis=1, tiled=True)  3.75 us
  transfers between devices with their start and end apart: 4, of which 2 were waited for; matrix products, arithmetic and copies ran while one was open for 9% of the time, Pallas kernels for 0%

commit v1 on v0

--- a/solution.py
+++ b/solution.py
@@ -87,7 +87,10 @@
         jnp.bfloat16
     )
     combined = jnp.dot(mixing, expert_out, preferred_element_type=jnp.float32).astype(jnp.bfloat16)
-    return lax.all_to_all(combined, "tp", split_axis=0, concat_axis=1, tiled=True)
+    return jnp.concatenate(
+        lax.all_to_all(jnp.stack(jnp.split(combined, lax.axis_size("tp"), axis=0)), "tp", 0, 0),
+        axis=1,
+    )
 
 
 def solution(mesh):

time: 140 us -> 140 us (level)
  no operation moved by 1% of the time
where the time goes in v1:
time: 140 us; the launch traced here: 139 us
  blocking collectives  39.1 us (28%)
  matrix products  33.7 us (24%)
  waiting for transfers between devices  33.1 us (24%)
  between operations  13.6 us (10%)
  starting transfers between devices  9.08 us (6%)
  local copies, waits for them, and re-layouts  6.33 us (5%)
  other arithmetic  4.46 us (3%)
    all_to_all x1, blocking collectives, body(): lax.all_to_all(outgoing, 'ep', split_axis=0, concat_axis=0, tiled=True)  33.4 us
    all_to_all x1, waiting for transfers between devices, body(): lax.all_to_all(flat_partial, 'ep', split_axis=0, concat_axis=0, tiled=True)  26 us
    dot_general x1, matrix products, body(): jnp.einsum('shcf,hfd->shcd', hidden_units, w_down, preferred_element_type...  11.5 us
    dot_general x1, matrix products, body(): jnp.einsum('shcd,hdf->shcf', received, w_up, preferred_element_type=jnp.f...  10.1 us
    dot_general x1, matrix products, body(): jnp.einsum('shcd,hdf->shcf', received, w_gate, preferred_element_type=jnp...  9.91 us
    reduce_scatter x1, waiting for transfers between devices, body(): lax.psum_scatter(up_sum, 'tp', scatter_dimension=0, tiled=True)  7.08 us
    all_to_all x1, starting transfers between devices, body(): lax.all_to_all(flat_partial, 'ep', split_axis=0, concat_axis=0, tiled=True)  5.74 us
    all_to_all x1, blocking collectives, body(): lax.all_to_all(jnp.stack(jnp.split(combined, lax.axis_size('tp'), axis=0)...  3.75 us
  transfers between devices with their start and end apart: 4, of which 2 were waited for; matrix products, arithmetic and copies ran while one was open for 9% of the time, Pallas kernels for 0%

profile of v1, /device:TPU:0, one launch (start us, length us, event | category | flops | bytes accessed | tf_op | source)
XLA Modules:
  0.0 139.3 jit_solution(17063286577456706128)
XLA Ops:
  6.5 0.0 copy-start
  6.5 0.9 fusion.16
  7.5 0.8 fusion.17
  8.3 0.1 reshape.52
  8.4 0.0 copy-done
  8.4 0.4 convolution_bitcast_fusion
  8.8 1.1 convolution_convert_fusion.2
  10.0 0.1 convert_element_type.70
  10.1 0.6 copy.29
  10.7 3.3 %all-to-all-start = ((bf16[4,2,2048]{2,0,1:T(4,128)(2,1)}), bf16[4,2,2048]{2,0,1:T(4,128)(2,1)S(1)}, u32[]{:S(2)}, u32[]{:S(2)}) async-start(bf16[4,2,2048]{2,0,1:T(4,128)(2,1)} %copy.29), calls=%async_computation | async-start | bytes 65536 | tf_op jit(solution)/shard_map/all_to_all | solution.py:44
  14.0 0.0 reduce-scatter.3.cloned.1.call-start
  14.1 0.8 eq.27
  14.8 0.1 fusion.20
  14.9 0.1 reduce_window_sum.11
  15.0 0.2 select_reduce_fusion.1
  15.2 0.1 reshape.51
  15.3 0.7 broadcast_add_fusion
  16.0 0.0 all-to-all-done
  16.0 0.1 add_reduce_fusion
  16.1 0.5 convolution_convert_fusion
  16.6 33.4 %all_to_all.31 = bf16[8,32,2048]{2,1,0:T(8,128)(2,1)S(1)} all-to-all(bf16[8,32,2048]{2,1,0:T(8,128)(2,1)S(1)} %bitcast.62), channel_id=1, replica_groups=mesh['groups'=2,'ep'=8,'tp'=2] {'ep'}, dimensions={0} | all-to-all | bytes 2097152 | tf_op jit(solution)/shard_map/all_to_all | solution.py:62
  50.0 0.6 copy.30
  50.6 0.0 copy-start.2
  50.6 9.9 %fusion.9 = f32[8,16,2,384]{3,0,2,1:T(8,128)S(1)} fusion(bf16[8,16,2,2048]{3,0,2,1:T(8,128)(2,1)S(1)} %bitcast.59, bf16[16,2048,384]{2,1,0:T(8,128)(2,1)} %param.16), kind=kOutput, calls=%fused_computation.9 | convolution fusion | flops 402653184 | bytes 26607616 | tf_op jit(solution)/shard_map/shcd,hdf->shcf/dot_general | solution.py:64
  60.5 0.9 copy.31
  61.3 0.0 reduce-scatter.3.cloned.1.call-update
  61.4 0.0 reduce-scatter.5.cloned.1.call-start
  61.4 0.0 copy-start.1
  61.4 10.1 %fusion.12 = f32[8,16,2,384]{3,0,2,1:T(8,128)S(1)} fusion(bf16[8,16,2,2048]{3,0,2,1:T(8,128)(2,1)S(1)} %bitcast.60, bf16[16,2048,384]{2,1,0:T(8,128)(2,1)} %param.17), kind=kOutput, calls=%fused_computation.10 | convolution fusion | flops 402653184 | bytes 26607616 | tf_op jit(solution)/shard_map/shcd,hdf->shcf/dot_general | solution.py:65
  71.6 0.0 copy-start.3
  71.6 0.9 copy.33
  72.4 0.0 reduce-scatter.5.cloned.1.call-update
  72.5 0.0 copy-done.2
  72.5 0.0 reduce-scatter.3.cloned.1.call-done
  72.6 7.1 %reduce-scatter.5.cloned.1.call-done = f32[4,16,2,384]{3,1,2,0:T(8,128)} async-done(((f32[8,16,2,384]{3,1,2,0:T(8,128)}), f32[4,16,2,384]{3,1,2,0:T(8,128)}) %reduce-scatter.5.cloned.1.call-update) | async-done | bytes 196624 | tf_op jit(solution)/shard_map/reduce_scatter | solution.py:68
  79.6 1.1 multiply_convert_fusion
  80.7 1.9 %all_gather.3 = bf16[8,16,2,384]{3,1,2,0:T(8,128)(2,1)S(1)} all-gather(bf16[4,16,2,384]{3,1,2,0:T(8,128)(2,1)S(1)} %multiply_convert_fusion), channel_id=1, replica_groups=mesh['groups'=2,'ep'=8,'tp'=2] {'tp'}, dimensions={0}, use_global_device_ids=true | all-gather | bytes 294912 | tf_op jit(solution)/shard_map/all_gather | solution.py:71
  82.7 11.5 %fusion.6 = bf16[16,8,2,2048]{3,1,2,0:T(8,128)(2,1)S(1)} fusion(bf16[16,384,2048]{2,1,0:T(8,128)(2,1)} %param.18, bf16[8,16,2,384]{3,1,2,0:T(8,128)(2,1)S(1)} %all_gather.3), kind=kOutput, calls=%fused_computation.6 | convolution fusion | flops 403177472 | bytes 26411008 | tf_op jit(solution)/shard_map/shcf,hfd->shcd/dot_general | solution.py:72
  94.2 1.6 %copy.36 = bf16[8,32,2048]{2,1,0:T(8,128)(2,1)} copy(bf16[8,32,2048]{2,0,1:T(8,128)(2,1)S(1)} %bitcast.61) | data formatting | bytes 2097152 | tf_op jit(solution)/shard_map/reshape | solution.py:75
  95.8 5.7 %all-to-all-start.2 = ((bf16[8,32,2048]{2,1,0:T(8,128)(2,1)}), bf16[8,32,2048]{2,1,0:T(8,128)(2,1)S(1)}, u32[]{:S(2)}, u32[]{:S(2)}) async-start(bf16[8,32,2048]{2,1,0:T(8,128)(2,1)} %copy.36), calls=%async_computation.4 | async-start | bytes 2097152 | tf_op jit(solution)/shard_map/all_to_all | solution.py:76
  101.5 0.1 reduce_sum.46
  101.6 0.1 fusion.22
  101.7 0.1 select_reduce_fusion
  101.8 26.0 %all-to-all-done.2 = bf16[8,32,2048]{2,1,0:T(8,128)(2,1)S(1)} async-done(((bf16[8,32,2048]{2,1,0:T(8,128)(2,1)}), bf16[8,32,2048]{2,1,0:T(8,128)(2,1)S(1)}, u32[]{:S(2)}, u32[]{:S(2)}) %all-to-all-start.2) | async-done | bytes 1048608 | tf_op jit(solution)/shard_map/all_to_all | solution.py:76
  127.8 0.1 add_convert_fusion
  127.9 0.2 convolution_convert_fusion.1
  128.1 3.7 %all_to_all.32 = bf16[2,4,2048]{2,1,0:T(4,128)(2,1)S(1)} all-to-all(bf16[2,4,2048]{2,1,0:T(4,128)(2,1)S(1)} %pad_maximum_fusion), channel_id=1, replica_groups=mesh['groups'=2,'ep'=8,'tp'=2] {'tp'}, dimensions={0} | all-to-all | bytes 65536 | tf_op jit(solution)/shard_map/all_to_all | solution.py:91
  131.9 0.6 copy.49
  (8 shorter events, 0.1 us)
Async XLA Ops:
  6.5 1.9 %copy-start = (f32[64,64]{1,0:T(8,128)S(1)}, f32[64,64]{1,0:T(8,128)}, u32[]{:S(2)}) copy-start(f32[64,64]{1,0:T(8,128)} %param.12) | copy-start | bytes 49156
  10.7 5.2 %all-to-all-start = ((bf16[4,2,2048]{2,0,1:T(4,128)(2,1)}), bf16[4,2,2048]{2,0,1:T(4,128)(2,1)S(1)}, u32[]{:S(2)}, u32[]{:S(2)}) async-start(bf16[4,2,2048]{2,0,1:T(4,128)(2,1)} %copy.29), calls=%async_computation | async-start | bytes 65536 | tf_op jit(solution)/shard_map/all_to_all | solution.py:44
  14.0 58.5 %reduce-scatter.3.cloned.1.call-start = ((), (), s32[]{:S(2)}) async-start(), calls=%async_computation.6 | async-start | bytes 589824 | tf_op jit(solution)/shard_map/reduce_scatter | solution.py:67
  50.6 21.9 %copy-start.2 = (f32[16,2,384]{2,1,0:T(2,128)S(1)}, f32[16,2,384]{2,1,0:T(2,128)}, u32[]{:S(2)}) copy-start(f32[16,2,384]{2,1,0:T(2,128)} %param.19) | copy-start | bytes 147460
  61.4 18.3 %reduce-scatter.5.cloned.1.call-start = ((), (), s32[]{:S(2)}) async-start(), calls=%async_computation.7 | async-start | bytes 589824 | tf_op jit(solution)/shard_map/reduce_scatter | solution.py:68
  61.4 71.1 %copy-start.1 = (f32[64,64]{1,0:T(8,128)S(1)}, f32[64,64]{1,0:T(8,128)}, u32[]{:S(2)}) copy-start(f32[64,64]{1,0:T(8,128)} %param.12) | copy-start | bytes 49156
  71.6 30.0 %copy-start.3 = (f32[8,8]{1,0:T(8,128)S(1)}, f32[8,8]{1,0:T(8,128)}, u32[]{:S(2)}) copy-start(f32[8,8]{1,0:T(8,128)} %param.15) | copy-start | bytes 772
  95.8 32.0 %all-to-all-start.2 = ((bf16[8,32,2048]{2,1,0:T(8,128)(2,1)}), bf16[8,32,2048]{2,1,0:T(8,128)(2,1)S(1)}, u32[]{:S(2)}, u32[]{:S(2)}) async-start(bf16[8,32,2048]{2,1,0:T(8,128)(2,1)} %copy.36), calls=%async_computation.4 | async-start | bytes 2097152 | tf_op jit(solution)/shard_map/all_to_all | solution.py:76
Sparse Core Ops, SparseCore 0:
  61.5 6.8 reduce-scatter.2
  72.6 7.0 reduce-scatter.4
